TPU v7x, 32 devices: a whole 2x2x4 slice. The times are simulated.
32 devices in a mesh: seq: 8 (over z, core), head: 4 (over y, x).
Axes of the slice: x: 2, y: 2, z: 4, core: 2. Of those that a mesh axis runs over, the one named last changes fastest.
Arguments:
- mixer_input: bfloat16 [2048, 4096], P('seq', 'head'), may hold values from -600 to 600
- gate_input: bfloat16 [2048, 4096], P('seq', 'head'), may hold values from -5 to 5
- b_proj: bfloat16 [2048, 128], P('seq'), may hold values from -0.5 to 0.5
- c_proj: bfloat16 [2048, 128], P('seq'), may hold values from -0.5 to 0.5
- decay_codes: int32 [64, 2048], P('head', 'seq'), may hold values from 1 to 4096
- decay_rates: float32 [64], P('head'), may hold values from 0 to 1
- skip_gain: float32 [64], P('head'), may hold values from 0.5 to 1.5
- norm_gain: float32 [4096], P('head'), may hold values from 0.5 to 1.5
- queries: bfloat16 [2048, 4096], P('seq', 'head'), may hold values from -5 to 5
- keys: bfloat16 [2048, 4096], P('seq', 'head'), may hold values from -5 to 5
Outputs:
- mamba_out: bfloat16 [2048, 4096], P('seq', 'head')
- attn_out: bfloat16 [2048, 4096], P('seq', 'head')
All inputs are finite; a program needn't handle non-finite values.
Results may differ from a plain program's by a relative error of at most 0.013.
Values may be sent and summed in bfloat16 or wider, within the bound.
No kernel may reach another device: no remote copies, remote signals or barrier semaphores. Data moves between devices by JAX's collectives and lax.ppermute only.
A program may use at most 64 MiB of HBM per device.

v0:
```python
import functools
import math
import jax
import jax.numpy as jnp
from jax import lax
from jax.sharding import PartitionSpec as P

HD = 128
CHANNELS_PER_HD = 64
BLOCK = 256
HIGH = lax.Precision.HIGHEST
NEG = -1e30


def carried_in(array, axis, combine, identity):
    devices, mine = (lax.axis_size(axis), lax.axis_index(axis))
    everything = jax.tree.map(
        lambda part, kind: lax.all_gather(part.astype(kind), axis),
        array,
        (jnp.bfloat16, jnp.bfloat16),
    )
    start = jax.tree.map(
        lambda part, zero: jnp.broadcast_to(jnp.asarray(zero, part.dtype), part.shape),
        array,
        identity,
    )

    def hop(k, before):
        reached = k < mine
        new = combine(
            before, jax.tree.map(lambda part, own: part[k].astype(own.dtype), everything, array)
        )
        return jax.tree.map(lambda a, b: jnp.where(reached, a, b), new, before)

    return lax.fori_loop(0, devices, hop, start)


def block_step(state_carry, inputs):
    x_block, b_block, c_block, decay_block = inputs
    running = jnp.cumsum(decay_block, axis=1)
    span = decay_block.shape[1]
    causal = (
        jnp.arange(span, dtype=jnp.int32)[:, None] >= jnp.arange(span, dtype=jnp.int32)[None, :]
    )
    log_gaps = jnp.where(causal[None, :, :], running[:, :, None] - running[:, None, :], NEG)
    decays = jnp.exp(log_gaps)
    match_strength = jnp.dot(c_block, b_block.T, preferred_element_type=jnp.float32)
    x_float = x_block.astype(jnp.float32)
    within = jnp.einsum(
        "hts,shp->thp", decays * match_strength[None, :, :], x_float, precision=HIGH
    )
    c_float = c_block.astype(jnp.float32)
    carried = jnp.exp(running).T[:, :, None] * jnp.einsum(
        "tn,hnp->thp", c_float, state_carry, precision=HIGH
    )
    to_end = jnp.exp(running[:, -1:] - running)
    updated_state = jnp.exp(running[:, -1])[:, None, None] * state_carry + jnp.einsum(
        "hs,sn,shp->hnp", to_end, b_block.astype(jnp.float32), x_float, precision=HIGH
    )
    return (updated_state, within + carried)


def local_scan(x_local, b_local, c_local, log_decay):
    tok_rows = x_local.shape[0]
    heads_local = log_decay.shape[0]
    block_count = tok_rows // BLOCK
    x_blocks = x_local.reshape(block_count, BLOCK, heads_local, CHANNELS_PER_HD)
    b_blocks = b_local.reshape(block_count, BLOCK, b_local.shape[1])
    c_blocks = c_local.reshape(block_count, BLOCK, c_local.shape[1])
    decay_blocks = log_decay.reshape(heads_local, block_count, BLOCK).transpose(1, 0, 2)
    initial = jnp.zeros((heads_local, b_local.shape[1], CHANNELS_PER_HD), jnp.float32)
    final_state, y_blocks = lax.scan(
        block_step, initial, (x_blocks, b_blocks, c_blocks, decay_blocks)
    )
    return (final_state, y_blocks.reshape(tok_rows, heads_local, CHANNELS_PER_HD))


def masked_scores(q_rows, q_pos, k_rows, k_pos):
    score_scale = 1.0 / math.sqrt(k_rows.shape[-1])
    scores = (
        jnp.einsum("qhd,khd->hqk", q_rows, k_rows, preferred_element_type=jnp.float32) * score_scale
    )
    visible = k_pos[None, None, :] <= q_pos[None, :, None]
    return (jnp.where(visible, scores, NEG), visible)


def online_update(group_state, q_rows, q_pos, k_rows, v_rows, k_pos):
    row_top, row_total, weighted_sum = group_state
    scores, visible = masked_scores(q_rows, q_pos, k_rows, k_pos)
    new_top = jnp.maximum(row_top, jnp.max(scores, axis=2))
    rescale = jnp.exp(row_top - new_top)
    weights = jnp.where(visible, jnp.exp(scores - new_top[:, :, None]), 0.0)
    row_total = row_total * rescale + jnp.sum(weights, axis=2)
    weighted_sum = weighted_sum * rescale[:, :, None] + jnp.einsum(
        "hqk,khd->hqd", weights.astype(jnp.bfloat16), v_rows, preferred_element_type=jnp.float32
    )
    return (new_top, row_total, weighted_sum)


def when_visible(state_update, group_state, q_pos, key_offset):
    return lax.cond(key_offset > q_pos[-1], lambda held: held, state_update, group_state)


def on_device(
    mixer_input,
    gate_input,
    b_proj,
    c_proj,
    decay_codes,
    decay_rates,
    skip_gain,
    norm_gain,
    queries,
    keys,
):
    tok_rows = mixer_input.shape[0]
    heads_local = decay_rates.shape[0]
    heads_att = queries.shape[1] // HD
    seq_rank = lax.axis_index("seq")
    own_positions = seq_rank * tok_rows + jnp.arange(tok_rows, dtype=jnp.int32)
    groups = [(queries, own_positions)]
    groups = [(q_rows.reshape(q_rows.shape[0], heads_att, HD), q_pos) for q_rows, q_pos in groups]
    log_decay = -decay_rates[:, None] * decay_codes.astype(jnp.float32)
    local_state, y_local = local_scan(mixer_input, b_proj, c_proj, log_decay)
    total_log = jnp.sum(log_decay, axis=1)

    def combine(earlier, later):
        return (earlier[0] + later[0], jnp.exp(later[0])[:, None, None] * earlier[1] + later[1])

    identity = (jnp.zeros_like(total_log), jnp.zeros_like(local_state))
    _, incoming = carried_in((total_log, local_state), "seq", combine, identity)
    running = jnp.cumsum(log_decay, axis=1)
    carried = jnp.einsum("tn,hnp->thp", c_proj.astype(jnp.float32), incoming, precision=HIGH)
    carried = carried * jnp.exp(running).T[:, :, None]
    x_float = mixer_input.reshape(tok_rows, heads_local, CHANNELS_PER_HD).astype(jnp.float32)
    ssm_out = (y_local + carried + skip_gain[None, :, None] * x_float).reshape(
        tok_rows, heads_local * CHANNELS_PER_HD
    )
    gated = ssm_out * jax.nn.silu(gate_input.astype(jnp.float32))
    squares = lax.psum(jnp.sum(gated * gated, axis=1), "head")
    channels = gated.shape[1] * lax.axis_size("head")
    mamba_out = (
        gated * lax.rsqrt(squares / channels + 1e-05)[:, None] * norm_gain[None, :]
    ).astype(jnp.bfloat16)
    initial = tuple(
        (
            (
                jnp.full((heads_att, q_pos.shape[0]), NEG, jnp.float32),
                jnp.zeros((heads_att, q_pos.shape[0]), jnp.float32),
                jnp.zeros((heads_att, q_pos.shape[0], HD), jnp.float32),
            )
            for _, q_pos in groups
        )
    )
    states = initial
    k_piece = lax.all_gather(keys, "seq", axis=0, tiled=True)
    v_piece = lax.all_gather(mamba_out, "seq", axis=0, tiled=True)
    row_count = k_piece.shape[0]
    block_rows = math.gcd(row_count, 512)

    def one_block(block_id, states):
        key_offset = block_id * block_rows
        k_rows = lax.dynamic_slice_in_dim(k_piece, block_id * block_rows, block_rows, 0).reshape(
            block_rows, heads_att, HD
        )
        v_rows = lax.dynamic_slice_in_dim(v_piece, block_id * block_rows, block_rows, 0).reshape(
            block_rows, heads_att, HD
        )
        k_pos = key_offset + jnp.arange(block_rows, dtype=jnp.int32)
        return tuple(
            (
                when_visible(
                    functools.partial(
                        online_update,
                        q_rows=group[0],
                        q_pos=group[1],
                        k_rows=k_rows,
                        v_rows=v_rows,
                        k_pos=k_pos,
                    ),
                    group_state,
                    group[1],
                    key_offset,
                )
                for group, group_state in zip(groups, states)
            )
        )

    finals = lax.fori_loop(0, row_count // block_rows, one_block, states)
    results = [(group_state[2], group_state[1]) for group_state in finals]
    rows_out = [
        (weighted / totals[:, :, None])
        .transpose(1, 0, 2)
        .reshape(weighted.shape[1], heads_att * HD)
        .astype(jnp.bfloat16)
        for weighted, totals in results
    ]
    attn_out = rows_out[0]
    return (mamba_out, attn_out)


def solution(mesh):
    in_specs = (
        P("seq", "head"),
        P("seq", "head"),
        P("seq", None),
        P("seq", None),
        P("head", "seq"),
        P("head"),
        P("head"),
        P("head"),
        P("seq", "head"),
        P("seq", "head"),
    )
    out_specs = (P("seq", "head"), P("seq", "head"))
    return jax.shard_map(
        on_device, mesh=mesh, in_specs=in_specs, out_specs=out_specs, check_vma=False
    )
```

profile of v0, /device:TPU:25, one launch (start us, length us, event | category | flops | bytes accessed | tf_op | source)
XLA Modules:
  0.0 200.4 jit_solution(12899004294406485471)
XLA Ops:
  11.2 2.2 %fusion.32 = bf16[16,128,64]{1,2,0:T(8,128)(2,1)} fusion(bf16[256,16,64]{0,2,1:T(8,128)(2,1)S(1)} %bitcast.92, f32[256,16]{0,1:T(8,128)S(1)} %get-tuple-element.482, f32[16]{0:T(128)S(1)} %exponential_multiply_fusion, bf16[256,128]{1,0:T(8,128)(2,1)} %param.18), kind=kOutput, calls=%fused_computation.45 | convolution fusion | flops 403439616 | bytes 868416 | tf_op jit(solution)/shard_map/while/body/eval_jaxpr/hs,sn,shp->hnp/dot_general | solution.py:57
  15.6 13.3 %all-reduce = bf16[128]{0:T(256)(128)(2,1)S(1)} all-reduce(bf16[128]{0:T(256)(128)(2,1)S(1)} %dynamic-update-slice), channel_id=2, replica_groups=mesh['seq'=8,'head'=4] {'seq'}, use_global_device_ids=true, to_apply=%add | all-reduce | flops 128 | bytes 512
  30.1 3.0 %fusion.23 = f32[256,16,64]{0,2,1:T(8,128)S(1)} fusion(bf16[256,16,64]{0,2,1:T(8,128)(2,1)S(1)} %bitcast.93, f32[256,256]{1,0:T(8,128)S(1)} %fusion.47, f32[16,256]{1,0:T(8,128)S(1)} %copy_bitcast_fusion.1, pred[256,256]{1,0:T(8,128)(4,1)S(1)} %iota_compare_fusion), kind=kOutput, calls=%fused_computation.32 | convolution fusion | flops 808452096 | bytes 1916928 | tf_op jit(solution)/shard_map/while/body/eval_jaxpr/hts,shp->thp/dot_general | solution.py:49
  33.7 9.1 %all-gather.10.cloned.1.call-done = bf16[128,128,64]{1,2,0:T(8,128)(2,1)} async-done(((bf16[16,128,64]{1,2,0:T(8,128)(2,1)}), bf16[128,128,64]{1,2,0:T(8,128)(2,1)}) %all-gather.10.cloned.1.call-update) | async-done | bytes 2097168 | tf_op jit(solution)/shard_map/all_gather | solution.py:18
  42.8 13.6 %while.37 = (s32[]{:T(128)}, f32[16,128,64]{2,1,0:T(8,128)S(1)}, s32[]{:T(128)}, bf16[8,16]{1,0:T(8,128)(2,1)S(1)}, bf16[8,16,128,64]{2,3,1,0:T(8,128)(2,1)}, /*index=5*/s32[]{:T(128)}, s32[]{:T(128)}) while((s32[]{:T(128)}, f32[16,128,64]{2,1,0:T(8,128)S(1)}, s32[]{:T(128)}, bf16[8,16]{1,0:T(8,128)(2,1)S(1)}, ...), condition=%wide.region_4.5_spmd.clone, body=%wide.region_3.4_spmd.clone.sunk | while | flops 655380 | bytes 2359569 | solution.py:35
  56.4 2.1 %fusion.28 = f32[256,16,64]{0,2,1:T(8,128)} fusion(f32[256,16,64]{0,2,1:T(8,128)S(1)} %fusion.30, f32[16,128,64]{2,1,0:T(8,128)S(1)} %get-tuple-element.383, bf16[256,16,64]{0,2,1:T(8,128)(2,1)S(1)} %bitcast.94, f32[16]{0:T(128)S(1)} %copy-done.5, f32[256,16]{0,1:T(8,128)S(1)} %get-tuple-element.483, bf16[256,128]{1,0:T(8,128)(2,1)S(1)} %copy-done), kind=kOutput, calls=%fused_computation.36 | convolution fusion | flops 403963904 | bytes 3227712 | tf_op jit(solution)/shard_map/tn,hnp->thp/dot_general | solution.py:133
  58.5 1.6 copy.59
  60.6 7.8 %psum.7 = f32[256]{0:T(256)S(1)} all-reduce(f32[256]{0:T(256)S(1)} %multiply_reduce_fusion), channel_id=1, replica_groups=mesh['seq'=8,'head'=4] {'head'}, use_global_device_ids=true, to_apply=%region_6.7 | all-reduce | flops 256 | bytes 2048 | tf_op jit(solution)/shard_map/psum | solution.py:140
  71.3 44.5 %all-gather.8.cloned.1.call-done = bf16[2048,1024]{1,0:T(8,128)(2,1)} async-done(((bf16[256,1024]{1,0:T(8,128)(2,1)}), bf16[2048,1024]{1,0:T(8,128)(2,1)}) %all-gather.8.cloned.1.call-update) | async-done | bytes 4194320 | tf_op jit(solution)/shard_map/all_gather | solution.py:157
  115.8 6.5 %copy.63 = bf16[2048,1024]{0,1:T(8,128)(2,1)} copy(bf16[2048,1024]{1,0:T(8,128)(2,1)} %all-gather.8.cloned.1.call-done) | data formatting | bytes 8388608 | tf_op jit(solution)/shard_map/while | solution.py:189
  122.3 41.8 %all-gather.6.cloned.1.call-done = bf16[2048,1024]{0,1:T(8,128)(2,1)} async-done(((bf16[256,1024]{0,1:T(8,128)(2,1)}), bf16[2048,1024]{0,1:T(8,128)(2,1)}) %all-gather.6.cloned.1.call-update) | async-done | bytes 4194320 | tf_op jit(solution)/shard_map/all_gather | solution.py:156
  164.2 28.6 %while.36 = (s32[]{:T(128)}, f32[8,256]{1,0:T(8,128)S(1)}, f32[8,256]{1,0:T(8,128)S(1)}, f32[8,256,128]{2,1,0:T(8,128)S(1)}, s32[256]{0:T(256)S(1)}, /*index=5*/...) while((s32[]{:T(128)}, f32[8,256]{1,0:T(8,128)S(1)}, ...), condition=%wide.region_12.13_spmd, body=%wide.region_7.12_spmd.sunk | while | flops 551162368 | bytes 22160680 | solution.py:189
  165.3 6.0 %conditional.2 = (f32[8,256]{1,0:T(8,128)S(1)}, f32[8,256]{1,0:T(8,128)S(1)}, f32[8,256,128]{2,1,0:T(8,128)S(1)}) conditional(s32[]{:T(128)} %convert_element_type.129, (s32[]{:T(128)}, s32[512]{0:T(512)S(1)}, s32[256]{0:T(256)S(1)}, bf16[2048,1024]{0,1:T(8,128)(2,1)}, bf16[256,8,128]{2,0,1:T(8,128)(2,1)S(1)}, /*index=5*/f32[8,256]{1,0:T(8,128)S(1)}, ...), branch_computations={%region_8.10_spmd, %region_11.11_spmd} | conditional | flops 551162368 | bytes 22142018 | solution.py:101
  165.5 1.7 constant_dynamic-slice_fusion
  169.2 2.1 %fusion.6 = f32[8,256,128]{2,1,0:T(8,128)S(1)} fusion(bf16[512,8,128]{0,2,1:T(8,128)(2,1)S(1)} %bitcast.91, f32[8,512,256]{2,1,0:T(8,128)S(1)} %get-tuple-element.477, f32[8,256]{1,0:T(8,128)S(1)} %max.5, pred[256,512]{0,1:T(8,128)(4,1)S(1)} %broadcast_compare_fusion, f32[8,256,128]{2,1,0:T(8,128)S(1)} %get-tuple-element.364, ...), kind=kOutput, calls=%fused_computation.7 | convolution fusion | flops 274202624 | bytes 7487488 | tf_op jit(solution)/shard_map/while/body/eval_jaxpr/cond/branch_0_fun/hqk,khd->hqd/dot_general | solution.py:94
  172.5 6.0 %conditional.2 = (f32[8,256]{1,0:T(8,128)S(1)}, f32[8,256]{1,0:T(8,128)S(1)}, f32[8,256,128]{2,1,0:T(8,128)S(1)}) conditional(s32[]{:T(128)} %convert_element_type.129, (s32[]{:T(128)}, s32[512]{0:T(512)S(1)}, s32[256]{0:T(256)S(1)}, bf16[2048,1024]{0,1:T(8,128)(2,1)}, bf16[256,8,128]{2,0,1:T(8,128)(2,1)S(1)}, /*index=5*/f32[8,256]{1,0:T(8,128)S(1)}, ...), branch_computations={%region_8.10_spmd, %region_11.11_spmd} | conditional | flops 551162368 | bytes 22142018 | solution.py:101
  172.7 1.7 constant_dynamic-slice_fusion
  176.3 2.1 %fusion.6 = f32[8,256,128]{2,1,0:T(8,128)S(1)} fusion(bf16[512,8,128]{0,2,1:T(8,128)(2,1)S(1)} %bitcast.91, f32[8,512,256]{2,1,0:T(8,128)S(1)} %get-tuple-element.477, f32[8,256]{1,0:T(8,128)S(1)} %max.5, pred[256,512]{0,1:T(8,128)(4,1)S(1)} %broadcast_compare_fusion, f32[8,256,128]{2,1,0:T(8,128)S(1)} %get-tuple-element.364, ...), kind=kOutput, calls=%fused_computation.7 | convolution fusion | flops 274202624 | bytes 7487488 | tf_op jit(solution)/shard_map/while/body/eval_jaxpr/cond/branch_0_fun/hqk,khd->hqd/dot_general | solution.py:94
  179.6 6.0 %conditional.2 = (f32[8,256]{1,0:T(8,128)S(1)}, f32[8,256]{1,0:T(8,128)S(1)}, f32[8,256,128]{2,1,0:T(8,128)S(1)}) conditional(s32[]{:T(128)} %convert_element_type.129, (s32[]{:T(128)}, s32[512]{0:T(512)S(1)}, s32[256]{0:T(256)S(1)}, bf16[2048,1024]{0,1:T(8,128)(2,1)}, bf16[256,8,128]{2,0,1:T(8,128)(2,1)S(1)}, /*index=5*/f32[8,256]{1,0:T(8,128)S(1)}, ...), branch_computations={%region_8.10_spmd, %region_11.11_spmd} | conditional | flops 551162368 | bytes 22142018 | solution.py:101
  179.8 1.7 constant_dynamic-slice_fusion
  183.5 2.1 %fusion.6 = f32[8,256,128]{2,1,0:T(8,128)S(1)} fusion(bf16[512,8,128]{0,2,1:T(8,128)(2,1)S(1)} %bitcast.91, f32[8,512,256]{2,1,0:T(8,128)S(1)} %get-tuple-element.477, f32[8,256]{1,0:T(8,128)S(1)} %max.5, pred[256,512]{0,1:T(8,128)(4,1)S(1)} %broadcast_compare_fusion, f32[8,256,128]{2,1,0:T(8,128)S(1)} %get-tuple-element.364, ...), kind=kOutput, calls=%fused_computation.7 | convolution fusion | flops 274202624 | bytes 7487488 | tf_op jit(solution)/shard_map/while/body/eval_jaxpr/cond/branch_0_fun/hqk,khd->hqd/dot_general | solution.py:94
  186.8 6.0 %conditional.2 = (f32[8,256]{1,0:T(8,128)S(1)}, f32[8,256]{1,0:T(8,128)S(1)}, f32[8,256,128]{2,1,0:T(8,128)S(1)}) conditional(s32[]{:T(128)} %convert_element_type.129, (s32[]{:T(128)}, s32[512]{0:T(512)S(1)}, s32[256]{0:T(256)S(1)}, bf16[2048,1024]{0,1:T(8,128)(2,1)}, bf16[256,8,128]{2,0,1:T(8,128)(2,1)S(1)}, /*index=5*/f32[8,256]{1,0:T(8,128)S(1)}, ...), branch_computations={%region_8.10_spmd, %region_11.11_spmd} | conditional | flops 551162368 | bytes 22142018 | solution.py:101
  187.0 1.7 constant_dynamic-slice_fusion
  190.6 2.1 %fusion.6 = f32[8,256,128]{2,1,0:T(8,128)S(1)} fusion(bf16[512,8,128]{0,2,1:T(8,128)(2,1)S(1)} %bitcast.91, f32[8,512,256]{2,1,0:T(8,128)S(1)} %get-tuple-element.477, f32[8,256]{1,0:T(8,128)S(1)} %max.5, pred[256,512]{0,1:T(8,128)(4,1)S(1)} %broadcast_compare_fusion, f32[8,256,128]{2,1,0:T(8,128)S(1)} %get-tuple-element.364, ...), kind=kOutput, calls=%fused_computation.7 | convolution fusion | flops 274202624 | bytes 7487488 | tf_op jit(solution)/shard_map/while/body/eval_jaxpr/cond/branch_0_fun/hqk,khd->hqd/dot_general | solution.py:94
  (117 shorter events, 35.6 us)
Async XLA Ops:
  7.2 21.9 %copy-start = (bf16[256,128]{1,0:T(8,128)(2,1)S(1)}, bf16[256,128]{1,0:T(8,128)(2,1)}, u32[]{:S(2)}) copy-start(bf16[256,128]{1,0:T(8,128)(2,1)} %param.19) | copy-start | bytes 196612
  7.2 35.6 %all-gather.10.cloned.1.call-start = ((), (), s32[]{:S(2)}) async-start(), calls=%async_computation.2 | async-start | bytes 2359296 | tf_op jit(solution)/shard_map/all_gather | solution.py:18
  13.4 102.4 %all-gather.8.cloned.1.call-start = ((), (), s32[]{:S(2)}) async-start(), calls=%async_computation.1 | async-start | bytes 4718592 | tf_op jit(solution)/shard_map/all_gather | solution.py:157
  42.8 13.6 %copy-start.5 = (f32[16]{0:T(128)S(1)}, f32[16]{0:T(128)}, u32[]{:S(2)}) copy-start(f32[16]{0:T(128)} %param.22) | copy-start | bytes 196
  56.4 3.8 %copy-start.1 = (bf16[256,1024]{1,0:T(8,128)(2,1)S(1)}, bf16[256,1024]{1,0:T(8,128)(2,1)}, u32[]{:S(2)}) copy-start(bf16[256,1024]{1,0:T(8,128)(2,1)} %param.17) | copy-start | bytes 1572868
  56.4 12.0 %copy-start.4 = (f32[1024]{0:T(1024)S(1)}, f32[1024]{0:T(1024)}, u32[]{:S(2)}) copy-start(f32[1024]{0:T(1024)} %param.23) | copy-start | bytes 12292
  58.5 11.3 %copy-start.2 = (bf16[256,1024]{1,0:T(8,128)(2,1)S(1)}, bf16[256,1024]{1,0:T(8,128)(2,1)}, u32[]{:S(2)}) copy-start(bf16[256,1024]{1,0:T(8,128)(2,1)} %param.25) | copy-start | bytes 1572868
  58.5 12.3 %copy-start.3 = (bf16[256,1024]{1,0:T(8,128)(2,1)S(1)}, bf16[256,1024]{1,0:T(8,128)(2,1)}, u32[]{:S(2)}) copy-start(bf16[256,1024]{1,0:T(8,128)(2,1)} %param.24) | copy-start | bytes 1572868
  69.5 94.6 %all-gather.6.cloned.1.call-start = ((), (), s32[]{:S(2)}) async-start(), calls=%async_computation | async-start | bytes 4718592 | tf_op jit(solution)/shard_map/all_gather | solution.py:156
Sparse Core Ops, SparseCore 0:
  13.5 29.2 all-gather.9
  69.7 46.0 all-gather.7
  118.0 46.0 all-gather.5
where the time goes:
time: 201 us; the launch traced here: 200 us
  waiting for transfers between devices  95.4 us (47%)
  local copies, waits for them, and re-layouts  32 us (16%)
  blocking collectives  21.1 us (10%)
  matrix products  21 us (10%)
  between operations  14.6 us (7%)
  other arithmetic  12.9 us (6%)
  loops' own time  3.13 us (2%)
    all_gather x1, waiting for transfers between devices, on_device(): v_piece = lax.all_gather(mamba_out, 'seq', axis=0, tiled=True)  44.5 us
    all_gather x1, waiting for transfers between devices, on_device(): k_piece = lax.all_gather(keys, 'seq', axis=0, tiled=True)  41.8 us
    unnamed x1, blocking collectives  13.3 us
    dynamic_slice x16, local copies, waits for them, and re-layouts, hop(): part[k].astype(own.dtype)  10.1 us
    all_gather x1, waiting for transfers between devices, carried_in(): lax.all_gather(part.astype(kind), axis)  9.1 us
    dot_general x4, matrix products, online_update(): jnp.einsum('hqk,khd->hqd', weights.astype(jnp.bfloat16), v_rows, preferre...  8.4 us
    psum x1, blocking collectives, on_device(): squares = lax.psum(jnp.sum(gated * gated, axis=1), 'head')  7.76 us
    while x2, local copies, waits for them, and re-layouts, on_device(): finals = lax.fori_loop(0, row_count // block_rows, one_block, states)  6.79 us
  transfers between devices with their start and end apart: 3, of which 3 were waited for; matrix products, arithmetic and copies ran while one was open for 7% of the time, Pallas kernels for 0%

commit v1 on v0

--- a/solution.py
+++ b/solution.py
@@ -153,8 +153,11 @@
         )
     )
     states = initial
-    k_piece = lax.all_gather(keys, "seq", axis=0, tiled=True)
-    v_piece = lax.all_gather(mamba_out, "seq", axis=0, tiled=True)
+    k_piece, v_piece = jnp.split(
+        lax.all_gather(jnp.concatenate([keys, mamba_out], axis=1), "seq", axis=0, tiled=True),
+        [keys.shape[1]],
+        axis=1,
+    )
     row_count = k_piece.shape[0]
     block_rows = math.gcd(row_count, 512)
 

time: 201 us -> 208 us (1.035)
  local copies, waits for them, and re-layouts: 32 us -> 43.4 us
  waiting for transfers between devices: 95.4 us -> 89.2 us
    while x2 -> x3, local copies, waits for them, and re-layouts: 6.79 us -> 13.3 us  [on_device(): finals = lax.fori_loop(0, row_count // block_rows, one_block, states)]
    all_gather x2 -> x1, waiting for transfers between devices: 86.3 us -> 80.1 us  [on_device(): lax.all_gather(jnp.concatenate([keys, mamba_out], axis=1), 'seq', axis=0,...]
    split x0 -> x1, local copies, waits for them, and re-layouts: none -> 5.9 us  [on_device(): jnp.split(lax.all_gather(jnp.concatenate([keys, mamba_out], axis=1), 'seq...]
  transfers between devices with their start and end apart: 3 -> 2, of which waited for: 3 -> 2; matrix products, arithmetic and copies ran while one was open for 7% -> 3% of each run, Pallas kernels for 0% -> 0%
where the time goes in v1:
time: 208 us; the launch traced here: 206 us
  waiting for transfers between devices  89.2 us (43%)
  local copies, waits for them, and re-layouts  43.4 us (21%)
  blocking collectives  21.3 us (10%)
  matrix products  21 us (10%)
  between operations  14.9 us (7%)
  other arithmetic  13.4 us (6%)
  loops' own time  3.12 us (2%)
    all_gather x1, waiting for transfers between devices, on_device(): lax.all_gather(jnp.concatenate([keys, mamba_out], axis=1), 'seq', axis=0,...  80.1 us
    unnamed x1, blocking collectives  13.3 us
    while x3, local copies, waits for them, and re-layouts, on_device(): finals = lax.fori_loop(0, row_count // block_rows, one_block, states)  13.3 us
    dynamic_slice x16, local copies, waits for them, and re-layouts, hop(): part[k].astype(own.dtype)  10.1 us
    all_gather x1, waiting for transfers between devices, carried_in(): lax.all_gather(part.astype(kind), axis)  9.09 us
    dot_general x4, matrix products, online_update(): jnp.einsum('hqk,khd->hqd', weights.astype(jnp.bfloat16), v_rows, preferre...  8.4 us
    psum x1, blocking collectives, on_device(): squares = lax.psum(jnp.sum(gated * gated, axis=1), 'head')  7.94 us
    dynamic_slice x4, local copies, waits for them, and re-layouts, one_block(): lax.dynamic_slice_in_dim(v_piece, block_id * block_rows, block_rows, 0)  6.76 us
  transfers between devices with their start and end apart: 2, of which 2 were waited for; matrix products, arithmetic and copies ran while one was open for 3% of the time, Pallas kernels for 0%

profile of v1, /device:TPU:25, one launch (start us, length us, event | category | flops | bytes accessed | tf_op | source)
XLA Modules:
  0.0 206.4 jit_solution(3087493953639364013)
XLA Ops:
  11.2 2.2 %fusion.32 = bf16[16,128,64]{1,2,0:T(8,128)(2,1)} fusion(bf16[256,16,64]{0,2,1:T(8,128)(2,1)S(1)} %bitcast.92, f32[256,16]{0,1:T(8,128)S(1)} %get-tuple-element.484, f32[16]{0:T(128)S(1)} %exponential_multiply_fusion, bf16[256,128]{1,0:T(8,128)(2,1)} %param.18), kind=kOutput, calls=%fused_computation.45 | convolution fusion | flops 403439616 | bytes 868416 | tf_op jit(solution)/shard_map/while/body/eval_jaxpr/hs,sn,shp->hnp/dot_general | solution.py:57
  15.7 13.3 %all-reduce = bf16[128]{0:T(256)(128)(2,1)S(1)} all-reduce(bf16[128]{0:T(256)(128)(2,1)S(1)} %dynamic-update-slice), channel_id=2, replica_groups=mesh['seq'=8,'head'=4] {'seq'}, use_global_device_ids=true, to_apply=%add | all-reduce | flops 128 | bytes 512
  30.1 3.0 %fusion.23 = f32[256,16,64]{0,2,1:T(8,128)S(1)} fusion(bf16[256,16,64]{0,2,1:T(8,128)(2,1)S(1)} %bitcast.93, f32[256,256]{1,0:T(8,128)S(1)} %fusion.48, f32[16,256]{1,0:T(8,128)S(1)} %copy_bitcast_fusion.1, pred[256,256]{1,0:T(8,128)(4,1)S(1)} %iota_compare_fusion), kind=kOutput, calls=%fused_computation.32 | convolution fusion | flops 808452096 | bytes 1916928 | tf_op jit(solution)/shard_map/while/body/eval_jaxpr/hts,shp->thp/dot_general | solution.py:49
  33.7 9.1 %all-gather.7.cloned.1.call-done = bf16[128,128,64]{1,2,0:T(8,128)(2,1)} async-done(((bf16[16,128,64]{1,2,0:T(8,128)(2,1)}), bf16[128,128,64]{1,2,0:T(8,128)(2,1)}) %all-gather.7.cloned.1.call-update) | async-done | bytes 2097168 | tf_op jit(solution)/shard_map/all_gather | solution.py:18
  42.8 13.5 %while.37 = (s32[]{:T(128)}, f32[16,128,64]{2,1,0:T(8,128)S(1)}, s32[]{:T(128)}, bf16[8,16]{1,0:T(8,128)(2,1)S(1)}, bf16[8,16,128,64]{2,3,1,0:T(8,128)(2,1)}, /*index=5*/s32[]{:T(128)}, s32[]{:T(128)}) while((s32[]{:T(128)}, f32[16,128,64]{2,1,0:T(8,128)S(1)}, s32[]{:T(128)}, bf16[8,16]{1,0:T(8,128)(2,1)S(1)}, ...), condition=%wide.region_4.5_spmd.clone, body=%wide.region_3.4_spmd.clone.sunk | while | flops 655380 | bytes 2359561 | solution.py:35
  56.4 2.1 %fusion.28 = f32[256,16,64]{0,2,1:T(8,128)} fusion(f32[256,16,64]{0,2,1:T(8,128)S(1)} %fusion.30, f32[16,128,64]{2,1,0:T(8,128)S(1)} %get-tuple-element.383, bf16[256,16,64]{0,2,1:T(8,128)(2,1)S(1)} %bitcast.94, f32[16]{0:T(128)S(1)} %copy-done.6, f32[256,16]{0,1:T(8,128)S(1)} %get-tuple-element.485, bf16[256,128]{1,0:T(8,128)(2,1)S(1)} %copy-done), kind=kOutput, calls=%fused_computation.36 | convolution fusion | flops 403963904 | bytes 3227712 | tf_op jit(solution)/shard_map/tn,hnp->thp/dot_general | solution.py:133
  60.6 7.9 %psum.7 = f32[256]{0:T(256)S(1)} all-reduce(f32[256]{0:T(256)S(1)} %multiply_reduce_fusion), channel_id=1, replica_groups=mesh['seq'=8,'head'=4] {'head'}, use_global_device_ids=true, to_apply=%region_6.7 | all-reduce | flops 256 | bytes 2048 | tf_op jit(solution)/shard_map/psum | solution.py:140
  70.7 80.1 %all-gather.5.cloned.1.call-done = bf16[2048,2048]{1,0:T(8,128)(2,1)} async-done(((bf16[256,2048]{1,0:T(8,128)(2,1)}), bf16[2048,2048]{1,0:T(8,128)(2,1)}) %all-gather.5.cloned.1.call-update) | async-done | bytes 8388624 | tf_op jit(solution)/shard_map/all_gather | solution.py:157
  150.8 5.9 %fusion.47 = (bf16[2048,1024]{1,0:T(8,128)(2,1)}, bf16[2048,1024]{1,0:T(8,128)(2,1)}) fusion(bf16[2048,2048]{1,0:T(8,128)(2,1)} %all-gather.5.cloned.1.call-done), kind=kLoop, calls=%fused_computation.77 | loop fusion | bytes 16777216 | tf_op jit(solution)/shard_map/split | solution.py:156
  156.7 6.5 %copy.61 = bf16[2048,1024]{0,1:T(8,128)(2,1)} copy(bf16[2048,1024]{1,0:T(8,128)(2,1)} %get-tuple-element.481) | data formatting | bytes 8388608 | tf_op jit(solution)/shard_map/while | solution.py:192
  163.2 6.5 %copy.63 = bf16[2048,1024]{0,1:T(8,128)(2,1)} copy(bf16[2048,1024]{1,0:T(8,128)(2,1)} %get-tuple-element.480) | data formatting | bytes 8388608 | tf_op jit(solution)/shard_map/while | solution.py:192
  169.8 28.6 %while.36 = (s32[]{:T(128)}, f32[8,256]{1,0:T(8,128)S(1)}, f32[8,256]{1,0:T(8,128)S(1)}, f32[8,256,128]{2,1,0:T(8,128)S(1)}, s32[256]{0:T(256)S(1)}, /*index=5*/...) while((s32[]{:T(128)}, f32[8,256]{1,0:T(8,128)S(1)}, ...), condition=%wide.region_12.13_spmd, body=%wide.region_7.12_spmd.sunk | while | flops 551162368 | bytes 22160680 | solution.py:192
  171.0 6.0 %conditional.2 = (f32[8,256]{1,0:T(8,128)S(1)}, f32[8,256]{1,0:T(8,128)S(1)}, f32[8,256,128]{2,1,0:T(8,128)S(1)}) conditional(s32[]{:T(128)} %convert_element_type.129, (s32[]{:T(128)}, s32[512]{0:T(512)S(1)}, s32[256]{0:T(256)S(1)}, bf16[2048,1024]{0,1:T(8,128)(2,1)}, bf16[256,8,128]{2,0,1:T(8,128)(2,1)S(1)}, /*index=5*/f32[8,256]{1,0:T(8,128)S(1)}, ...), branch_computations={%region_8.10_spmd, %region_11.11_spmd} | conditional | flops 551162368 | bytes 22142018 | solution.py:101
  171.0 1.7 constant_dynamic-slice_fusion
  174.8 2.1 %fusion.6 = f32[8,256,128]{2,1,0:T(8,128)S(1)} fusion(bf16[512,8,128]{0,2,1:T(8,128)(2,1)S(1)} %bitcast.91, f32[8,512,256]{2,1,0:T(8,128)S(1)} %get-tuple-element.477, f32[8,256]{1,0:T(8,128)S(1)} %max.5, pred[256,512]{0,1:T(8,128)(4,1)S(1)} %broadcast_compare_fusion, f32[8,256,128]{2,1,0:T(8,128)S(1)} %get-tuple-element.364, ...), kind=kOutput, calls=%fused_computation.7 | convolution fusion | flops 274202624 | bytes 7487488 | tf_op jit(solution)/shard_map/while/body/eval_jaxpr/cond/branch_0_fun/hqk,khd->hqd/dot_general | solution.py:94
  178.1 6.0 %conditional.2 = (f32[8,256]{1,0:T(8,128)S(1)}, f32[8,256]{1,0:T(8,128)S(1)}, f32[8,256,128]{2,1,0:T(8,128)S(1)}) conditional(s32[]{:T(128)} %convert_element_type.129, (s32[]{:T(128)}, s32[512]{0:T(512)S(1)}, s32[256]{0:T(256)S(1)}, bf16[2048,1024]{0,1:T(8,128)(2,1)}, bf16[256,8,128]{2,0,1:T(8,128)(2,1)S(1)}, /*index=5*/f32[8,256]{1,0:T(8,128)S(1)}, ...), branch_computations={%region_8.10_spmd, %region_11.11_spmd} | conditional | flops 551162368 | bytes 22142018 | solution.py:101
  178.1 1.7 constant_dynamic-slice_fusion
  182.0 2.1 %fusion.6 = f32[8,256,128]{2,1,0:T(8,128)S(1)} fusion(bf16[512,8,128]{0,2,1:T(8,128)(2,1)S(1)} %bitcast.91, f32[8,512,256]{2,1,0:T(8,128)S(1)} %get-tuple-element.477, f32[8,256]{1,0:T(8,128)S(1)} %max.5, pred[256,512]{0,1:T(8,128)(4,1)S(1)} %broadcast_compare_fusion, f32[8,256,128]{2,1,0:T(8,128)S(1)} %get-tuple-element.364, ...), kind=kOutput, calls=%fused_computation.7 | convolution fusion | flops 274202624 | bytes 7487488 | tf_op jit(solution)/shard_map/while/body/eval_jaxpr/cond/branch_0_fun/hqk,khd->hqd/dot_general | solution.py:94
  185.3 6.0 %conditional.2 = (f32[8,256]{1,0:T(8,128)S(1)}, f32[8,256]{1,0:T(8,128)S(1)}, f32[8,256,128]{2,1,0:T(8,128)S(1)}) conditional(s32[]{:T(128)} %convert_element_type.129, (s32[]{:T(128)}, s32[512]{0:T(512)S(1)}, s32[256]{0:T(256)S(1)}, bf16[2048,1024]{0,1:T(8,128)(2,1)}, bf16[256,8,128]{2,0,1:T(8,128)(2,1)S(1)}, /*index=5*/f32[8,256]{1,0:T(8,128)S(1)}, ...), branch_computations={%region_8.10_spmd, %region_11.11_spmd} | conditional | flops 551162368 | bytes 22142018 | solution.py:101
  185.3 1.7 constant_dynamic-slice_fusion
  189.1 2.1 %fusion.6 = f32[8,256,128]{2,1,0:T(8,128)S(1)} fusion(bf16[512,8,128]{0,2,1:T(8,128)(2,1)S(1)} %bitcast.91, f32[8,512,256]{2,1,0:T(8,128)S(1)} %get-tuple-element.477, f32[8,256]{1,0:T(8,128)S(1)} %max.5, pred[256,512]{0,1:T(8,128)(4,1)S(1)} %broadcast_compare_fusion, f32[8,256,128]{2,1,0:T(8,128)S(1)} %get-tuple-element.364, ...), kind=kOutput, calls=%fused_computation.7 | convolution fusion | flops 274202624 | bytes 7487488 | tf_op jit(solution)/shard_map/while/body/eval_jaxpr/cond/branch_0_fun/hqk,khd->hqd/dot_general | solution.py:94
  192.4 6.0 %conditional.2 = (f32[8,256]{1,0:T(8,128)S(1)}, f32[8,256]{1,0:T(8,128)S(1)}, f32[8,256,128]{2,1,0:T(8,128)S(1)}) conditional(s32[]{:T(128)} %convert_element_type.129, (s32[]{:T(128)}, s32[512]{0:T(512)S(1)}, s32[256]{0:T(256)S(1)}, bf16[2048,1024]{0,1:T(8,128)(2,1)}, bf16[256,8,128]{2,0,1:T(8,128)(2,1)S(1)}, /*index=5*/f32[8,256]{1,0:T(8,128)S(1)}, ...), branch_computations={%region_8.10_spmd, %region_11.11_spmd} | conditional | flops 551162368 | bytes 22142018 | solution.py:101
  192.4 1.7 constant_dynamic-slice_fusion
  196.2 2.1 %fusion.6 = f32[8,256,128]{2,1,0:T(8,128)S(1)} fusion(bf16[512,8,128]{0,2,1:T(8,128)(2,1)S(1)} %bitcast.91, f32[8,512,256]{2,1,0:T(8,128)S(1)} %get-tuple-element.477, f32[8,256]{1,0:T(8,128)S(1)} %max.5, pred[256,512]{0,1:T(8,128)(4,1)S(1)} %broadcast_compare_fusion, f32[8,256,128]{2,1,0:T(8,128)S(1)} %get-tuple-element.364, ...), kind=kOutput, calls=%fused_computation.7 | convolution fusion | flops 274202624 | bytes 7487488 | tf_op jit(solution)/shard_map/while/body/eval_jaxpr/cond/branch_0_fun/hqk,khd->hqd/dot_general | solution.py:94
  (118 shorter events, 36.5 us)
Async XLA Ops:
  7.2 21.9 %copy-start = (bf16[256,128]{1,0:T(8,128)(2,1)S(1)}, bf16[256,128]{1,0:T(8,128)(2,1)}, u32[]{:S(2)}) copy-start(bf16[256,128]{1,0:T(8,128)(2,1)} %param.19) | copy-start | bytes 196612
  7.2 35.6 %all-gather.7.cloned.1.call-start = ((), (), s32[]{:S(2)}) async-start(), calls=%async_computation.1 | async-start | bytes 2359296 | tf_op jit(solution)/shard_map/all_gather | solution.py:18
  13.4 137.4 %all-gather.5.cloned.1.call-start = ((), (), s32[]{:S(2)}) async-start(), calls=%async_computation | async-start | bytes 9437184 | tf_op jit(solution)/shard_map/all_gather | solution.py:157
  42.8 13.6 %copy-start.6 = (f32[16]{0:T(128)S(1)}, f32[16]{0:T(128)}, u32[]{:S(2)}) copy-start(f32[16]{0:T(128)} %param.22) | copy-start | bytes 196
  56.4 3.8 %copy-start.1 = (bf16[256,1024]{1,0:T(8,128)(2,1)S(1)}, bf16[256,1024]{1,0:T(8,128)(2,1)}, u32[]{:S(2)}) copy-start(bf16[256,1024]{1,0:T(8,128)(2,1)} %param.17) | copy-start | bytes 1572868
  56.4 12.1 %copy-start.5 = (f32[1024]{0:T(1024)S(1)}, f32[1024]{0:T(1024)}, u32[]{:S(2)}) copy-start(f32[1024]{0:T(1024)} %param.23) | copy-start | bytes 12292
  58.5 10.4 %copy-start.4 = (bf16[256,1024]{1,0:T(8,128)(2,1)S(1)}, bf16[256,1024]{1,0:T(8,128)(2,1)}, u32[]{:S(2)}) copy-start(bf16[256,1024]{1,0:T(8,128)(2,1)} %param.25) | copy-start | bytes 1572868
  58.5 11.7 %copy-start.3 = (bf16[256,1024]{1,0:T(8,128)(2,1)S(1)}, bf16[256,1024]{1,0:T(8,128)(2,1)}, u32[]{:S(2)}) copy-start(bf16[256,1024]{1,0:T(8,128)(2,1)} %param.24) | copy-start | bytes 1572868
  68.9 87.8 %copy-start.2 = (bf16[256,1024]{1,0:T(8,128)(2,1)}, bf16[256,1024]{1,0:T(8,128)(2,1)S(1)}, u32[]{:S(2)}) copy-start(bf16[256,1024]{1,0:T(8,128)(2,1)S(1)} %multiply_convert_fusion) | copy-start | bytes 1572868
Sparse Core Ops, SparseCore 0:
  13.6 29.2 all-gather.6
  70.3 80.4 all-gather.4
